TPU v7x, 512 devices: a whole 4x8x8 slice. The times are simulated.
512 devices in a mesh: rep: 16 (over y, core), dom: 32 (over x, z).
Axes of the slice: x: 4, y: 8, z: 8, core: 2. Of those that a mesh axis runs over, the one named last changes fastest.
Arguments:
- features: bfloat16 [524288, 768], P(('rep', 'dom')), may hold values from -24 to 24
- cotangent: bfloat16 [524288, 1024], P(('rep', 'dom')), may hold values from -0.008239746 to 0.008239746
- w_self: bfloat16 [768, 1024], P('dom'), may hold values from -0.21875 to 0.21875
- w_neigh: bfloat16 [768, 1024], P('dom'), may hold values from -0.21875 to 0.21875
- tile_vals: bfloat16 [16384, 128, 128], P(('rep', 'dom')), may hold values from 0 to 0.088378906
- tile_src: int32 [16384], P(('rep', 'dom')), may hold values from 0 to 7
- tile_peer: int32 [16384], P(('rep', 'dom')), may hold values from 0 to 31
- in_block: int32 [16384], P(('rep', 'dom')), may hold values from 0 to 7
Outputs:
- grad_self: float32 [768, 1024], P('dom')
- grad_neigh: float32 [768, 1024], P('dom')
Inputs may be any that keep to these rules, and one draw needn't show every extreme that they name: `in_block`: all tiles that one partition sends to one receiving partition land in the same receiver block.
All inputs are finite; a program needn't handle non-finite values.
Results may differ from a plain program's by a relative error of at most 0.023.
Values may be sent and summed in bfloat16 or wider, within the bound.
A program may use at most 128 MiB of HBM per device.

v0:
```python
import jax
import jax.numpy as jnp
from jax import lax
from jax.sharding import Mesh
from jax.sharding import PartitionSpec as P

DOM = ("dom_0", "dom_1")
REP_DOM = ("rep", "dom_0", "dom_1")


def side_by_side(arrays, axis, dim, along):
    both = jnp.concatenate(arrays, axis=along)
    out, at, outs = (lax.all_gather(both, axis, axis=dim, tiled=True), 0, [])
    for a in arrays:
        outs.append(lax.slice_in_dim(out, at, at + a.shape[along], axis=along))
        at += a.shape[along]
    return tuple(outs)


def own_rows(terms, axes):
    total = terms.astype(jnp.bfloat16)
    for axis in axes:
        total = lax.psum_scatter(total, axis, scatter_dimension=0, tiled=True)
    return total.astype(jnp.float32)


def over_pieces(x, axis):
    return lax.all_gather(x, axis).astype(jnp.float32).sum(0)


def gelu_tanh(value):
    return jax.nn.gelu(value, approximate=True)


def add_product(left, total, piece):
    return total + jnp.dot(left, piece, preferred_element_type=jnp.float32)


def shards(features, cotangent, w_self, w_neigh, tile_vals, tile_src, tile_peer, in_block):
    dom_size = lax.axis_size(DOM)
    block = tile_vals.shape[1]
    width = features.shape[1]
    hidden = w_self.shape[1]
    block_count = features.shape[0] // block
    blocks = features.reshape(block_count, block, width)
    picked = blocks[tile_src]
    product = jnp.einsum("tij,tjf->tif", tile_vals, picked, preferred_element_type=jnp.float32)
    to_peer = (tile_peer[:, None] == jnp.arange(dom_size, dtype=jnp.int32)[None, :]).astype(
        jnp.float32
    )
    slots = jnp.einsum("tp,tif->pif", to_peer, product, precision=lax.Precision.HIGH).astype(
        jnp.bfloat16
    )
    empty = jnp.zeros((features.shape[0], hidden), jnp.float32)
    into_block = (in_block[:, None] == jnp.arange(block_count, dtype=jnp.int32)[None, :]).astype(
        jnp.bfloat16
    )
    received = lax.all_to_all(slots, DOM, split_axis=0, concat_axis=0, tiled=True)
    aggregate = jnp.einsum("sk,sif->kif", into_block, received, preferred_element_type=jnp.float32)
    aggregate = aggregate.reshape(features.shape[0], width).astype(jnp.bfloat16)
    total = empty
    pieces = side_by_side((w_self, w_neigh), DOM, 0, 1)
    total = add_product(features, total, pieces[0])
    preact = add_product(aggregate, total, pieces[1])
    _, pull = jax.vjp(gelu_tanh, preact)
    grad_pre = pull(cotangent.astype(jnp.float32))[0].astype(jnp.bfloat16)
    contract = (((0,), (0,)), ((), ()))
    self_term = lax.dot_general(features, grad_pre, contract, preferred_element_type=jnp.float32)
    neigh_term = lax.dot_general(aggregate, grad_pre, contract, preferred_element_type=jnp.float32)
    shares = own_rows(jnp.concatenate([self_term, neigh_term], axis=1), DOM)
    totals = over_pieces(shares.astype(jnp.bfloat16), "rep").astype(jnp.float32)
    return (totals[:, :hidden], totals[:, hidden:])


def solution(mesh):
    split = Mesh(mesh.devices.reshape(mesh.shape["rep"], 4, 8), ("rep", "dom_0", "dom_1"))
    placed = (
        P(REP_DOM, None),
        P(REP_DOM, None),
        P(DOM, None),
        P(DOM, None),
        P(REP_DOM, None, None),
        P(REP_DOM),
        P(REP_DOM),
        P(REP_DOM),
    )
    return jax.shard_map(
        shards, mesh=split, in_specs=placed, out_specs=(P(DOM, None), P(DOM, None)), check_vma=False
    )
```

profile of v0, /device:TPU:1, one launch (start us, length us, event | category | flops | bytes accessed | tf_op | source)
XLA Modules:
  0.0 386.5 jit_solution(7994320683611177807)
XLA Ops:
  7.2 0.8 compare_select_fusion
  8.0 0.6 copy-done
  8.6 3.5 gather_fusion
  12.1 9.2 %convolution_bitcast_fusion = f32[32,128,768]{1,2,0:T(8,128)} fusion(bf16[32,128,768]{2,1,0:T(8,128)(2,1)} %gather_fusion, bf16[32,128,128]{2,1,0:T(8,128)(2,1)S(1)} %copy-done.2), kind=kOutput, calls=%fused_computation.7 | convolution fusion | flops 805306368 | bytes 19922944 | tf_op jit(solution)/shard_map/tij,tjf->tif/dot_general | solution.py:47
  21.3 12.9 %copy.28 = f32[32,128,768]{2,0,1:T(8,128)} copy(f32[32,128,768]{1,2,0:T(8,128)} %convolution_bitcast_fusion) | data formatting | bytes 25165824 | tf_op jit(solution)/shard_map/tij,tjf->tif/dot_general | solution.py:47
  34.3 8.3 %convolution_convert_fusion = bf16[32,128,768]{2,0,1:T(8,128)(2,1)S(1)} fusion(f32[32,128,768]{2,0,1:T(8,128)} %copy.28, s32[32]{0:T(128)S(1)} %copy-done.5), kind=kOutput, calls=%fused_computation.19 | convolution fusion | flops 607126528 | bytes 18874496 | tf_op jit(solution)/shard_map/tp,tif->pif/dot_general | solution.py:51
  42.6 6.2 %copy.29 = bf16[32,128,768]{2,1,0:T(8,128)(2,1)} copy(bf16[32,128,768]{2,0,1:T(8,128)(2,1)S(1)} %convolution_convert_fusion) | data formatting | bytes 12582912 | tf_op jit(solution)/shard_map/convert_element_type | solution.py:51
  48.8 13.9 %all-to-all-start = ((bf16[32,128,768]{2,1,0:T(8,128)(2,1)}), bf16[32,128,768]{2,1,0:T(8,128)(2,1)}, u32[]{:S(2)}, u32[]{:S(2)}) async-start(bf16[32,128,768]{2,1,0:T(8,128)(2,1)} %copy.29), calls=%async_computation | async-start | bytes 12582912 | tf_op jit(solution)/shard_map/all_to_all | solution.py:58
  62.7 0.0 all-gather.4.cloned.1.call-start
  62.8 0.6 pad_maximum_fusion.1
  63.5 0.0 all-gather.4.cloned.1.call-update
  63.5 0.2 reduce-scatter.7.cloned.1.call-start
  63.7 4.0 %copy.26 = bf16[1024,1024]{0,1:T(8,128)(2,1)} copy(bf16[1024,1024]{1,0:T(8,128)(2,1)} %param.9) | data formatting | bytes 4194304 | tf_op args[1]
  67.7 152.4 %all-to-all-done = bf16[32,128,768]{2,1,0:T(8,128)(2,1)} async-done(((bf16[32,128,768]{2,1,0:T(8,128)(2,1)}), bf16[32,128,768]{2,1,0:T(8,128)(2,1)}, u32[]{:S(2)}, u32[]{:S(2)}) %all-to-all-start) | async-done | bytes 6291488 | tf_op jit(solution)/shard_map/all_to_all | solution.py:58
  220.1 7.3 %fusion.12 = bf16[8,128,768]{2,0,1:T(8,128)(2,1)S(1)} fusion(bf16[32,128,768]{2,1,0:T(8,128)(2,1)} %all-to-all-done, s32[32]{0:T(128)S(1)} %copy-done.6), kind=kOutput, calls=%fused_computation.22 | convolution fusion | flops 51118336 | bytes 7864448 | tf_op jit(solution)/shard_map/sk,sif->kif/dot_general | solution.py:59
  227.5 0.3 copy.31
  227.8 0.0 all-gather.4.cloned.1.call-done
  227.8 3.4 fusion.15
  231.3 5.2 %fusion.4 = bf16[1024,1024]{0,1:T(8,128)(2,1)S(1)} fusion(bf16[1024,1024]{0,1:T(8,128)(2,1)S(1)} %copy-done.1, f32[1024,1024]{0,1:T(8,128)S(1)} %fusion.15, bf16[1024,768]{1,0:T(8,128)(2,1)S(1)} %copy-done, bf16[768,2048]{1,0:T(8,128)(2,1)S(1)} %copy-done.7), kind=kOutput, calls=%fused_computation.10 | convolution fusion | flops 1633681408 | bytes 11534336 | tf_op jit(solution)/shard_map/dot_general | solution.py:36
  236.4 1.8 convolution_convert_fusion.1
  238.2 1.8 fusion.18
  240.0 1.9 pad_maximum_fusion
  241.9 4.7 %copy.38 = bf16[768,2048]{1,0:T(8,128)(2,1)} copy(bf16[768,2048]{0,1:T(8,128)(2,1)} %pad_maximum_fusion) | data formatting | bytes 6291456
  246.6 0.0 reduce-scatter.7.cloned.1.call-update
  246.6 0.0 reduce-scatter.9.cloned.1.call-start
  246.7 44.6 %reduce-scatter.7.cloned.1.call-done = bf16[192,2048]{1,0:T(8,128)(2,1)} async-done(((bf16[768,2048]{1,0:T(8,128)(2,1)}), bf16[192,2048]{1,0:T(8,128)(2,1)}) %reduce-scatter.7.cloned.1.call-update) | async-done | bytes 786448
  291.3 0.0 reduce-scatter.9.cloned.1.call-update
  291.3 0.0 all-gather.6.cloned.1.call-start
  291.4 39.5 %reduce-scatter.9.cloned.1.call-done = bf16[24,2048]{1,0:T(8,128)(2,1)} async-done(((bf16[192,2048]{1,0:T(8,128)(2,1)}), bf16[24,2048]{1,0:T(8,128)(2,1)}) %reduce-scatter.9.cloned.1.call-update) | async-done | bytes 98320 | tf_op jit(solution)/shard_map/reduce_scatter | solution.py:23
  330.8 46.7 %all-gather.6.cloned.1.call-done = bf16[384,2048]{1,0:T(8,128)(2,1)} async-done(((bf16[24,2048]{1,0:T(8,128)(2,1)}), bf16[384,2048]{1,0:T(8,128)(2,1)}) %all-gather.6.cloned.1.call-update) | async-done | bytes 1572880 | tf_op jit(solution)/shard_map/all_gather | solution.py:28
  377.6 1.7 convert_reduce_fusion
  379.2 0.7 fusion.25
  (17 shorter events, 0.1 us)
Async XLA Ops:
  7.2 1.4 copy-start
  8.6 3.5 copy-start.2
  21.3 12.9 %copy-start.5 = (s32[32]{0:T(128)S(1)}, s32[32]{0:T(128)}, u32[]{:S(2)}) copy-start(s32[32]{0:T(128)} %param.14) | copy-start | bytes 388
  48.8 14.0 %copy-start.3 = (bf16[24,1024]{1,0:T(8,128)(2,1)S(1)}, bf16[24,1024]{1,0:T(8,128)(2,1)}, u32[]{:S(2)}) copy-start(bf16[24,1024]{1,0:T(8,128)(2,1)} %param.11) | copy-start | bytes 147460
  48.8 14.0 %copy-start.4 = (bf16[24,1024]{1,0:T(8,128)(2,1)S(1)}, bf16[24,1024]{1,0:T(8,128)(2,1)}, u32[]{:S(2)}) copy-start(bf16[24,1024]{1,0:T(8,128)(2,1)} %param.10) | copy-start | bytes 147460
  48.8 171.3 %all-to-all-start = ((bf16[32,128,768]{2,1,0:T(8,128)(2,1)}), bf16[32,128,768]{2,1,0:T(8,128)(2,1)}, u32[]{:S(2)}, u32[]{:S(2)}) async-start(bf16[32,128,768]{2,1,0:T(8,128)(2,1)} %copy.29), calls=%async_computation | async-start | bytes 12582912 | tf_op jit(solution)/shard_map/all_to_all | solution.py:58
  62.7 157.4 %copy-start.6 = (s32[32]{0:T(128)S(1)}, s32[32]{0:T(128)}, u32[]{:S(2)}) copy-start(s32[32]{0:T(128)} %param.15) | copy-start | bytes 388
  62.7 165.0 %all-gather.4.cloned.1.call-start = ((), (), s32[]{:S(2)}) async-start(), calls=%async_computation.3 | async-start | bytes 3244032 | tf_op jit(solution)/shard_map/all_gather | solution.py:13
  63.5 227.8 %reduce-scatter.7.cloned.1.call-start = ((), (), s32[]{:S(2)}) async-start(), calls=%async_computation.5 | async-start | bytes 3932160
  227.8 3.5 copy-start.1
  227.8 3.5 copy-start.7
  246.6 84.2 %reduce-scatter.9.cloned.1.call-start = ((), (), s32[]{:S(2)}) async-start(), calls=%async_computation.6 | async-start | bytes 884736 | tf_op jit(solution)/shard_map/reduce_scatter | solution.py:23
  291.3 86.2 %all-gather.6.cloned.1.call-start = ((), (), s32[]{:S(2)}) async-start(), calls=%async_computation.4 | async-start | bytes 1671168 | tf_op jit(solution)/shard_map/all_gather | solution.py:28
Sparse Core Ops, SparseCore 0:
  67.3 135.9 all-gather.3
  246.7 44.5 reduce-scatter.6
  294.1 36.6 reduce-scatter.8
  332.8 44.7 all-gather.5
where the time goes:
time: 387 us; the launch traced here: 386 us
  waiting for transfers between devices  283 us (73%)
  matrix products  37 us (10%)
  local copies, waits for them, and re-layouts  32.9 us (9%)
  starting transfers between devices  14.3 us (4%)
  between operations  13.9 us (4%)
  other arithmetic  4.99 us (1%)
    all_to_all x1, waiting for transfers between devices, shards(): lax.all_to_all(slots, DOM, split_axis=0, concat_axis=0, tiled=True)  152 us
    all_gather x1, waiting for transfers between devices, over_pieces(): return lax.all_gather(x, axis).astype(jnp.float32).sum(0)  46.7 us
    unnamed x5, waiting for transfers between devices  44.7 us
    reduce_scatter x1, waiting for transfers between devices, own_rows(): total = lax.psum_scatter(total, axis, scatter_dimension=0, tiled=True)  39.5 us
    all_to_all x1, starting transfers between devices, shards(): lax.all_to_all(slots, DOM, split_axis=0, concat_axis=0, tiled=True)  13.9 us
    dot_general x1, local copies, waits for them, and re-layouts, shards(): jnp.einsum('tij,tjf->tif', tile_vals, picked, preferred_element_type=jnp....  12.9 us
    unnamed x18, local copies, waits for them, and re-layouts  9.31 us
    dot_general x1, matrix products, shards(): jnp.einsum('tij,tjf->tif', tile_vals, picked, preferred_element_type=jnp....  9.18 us
  transfers between devices with their start and end apart: 5, of which 4 were waited for; matrix products, arithmetic and copies ran while one was open for 3% of the time, Pallas kernels for 0%

commit v1 on v0

v1 whole, which is shorter than its diff:
```python
import functools

import jax
import jax.numpy as jnp
from jax import lax
from jax.experimental import pallas as pl
from jax.experimental.pallas import tpu as pltpu
from jax.sharding import Mesh
from jax.sharding import PartitionSpec as P

AXES = ("y", "c", "x", "z")
SIZES = (8, 2, 4, 8)
NY, NC, NX, NZ = SIZES
NDOM = NX * NZ
MESH = pl.DeviceIdType.MESH
VMEM_BYTES = 60 * 1024 * 1024
F32 = jnp.float32
BF16 = jnp.bfloat16

DIST = (4, 3, 3, 2, 2, 1, 1)
ITEMS = []
for _i, _d in enumerate(DIST):
    ITEMS += [(_i % 2, _d), (1 - _i % 2, -_d)]
ITEMS += [(0, 0), (1, 0)]


def position():
    return tuple(lax.axis_index(a) for a in AXES)


def moved(me, axis, by):
    return tuple(
        lax.rem(m + (by % SIZES[axis]), SIZES[axis]) if a == axis else m
        for a, m in enumerate(me)
    )


def greet(me):
    barrier = pltpu.get_barrier_semaphore()
    count = 0
    for axis, size in enumerate(SIZES):
        for by in range(1, size):
            pl.semaphore_signal(
                barrier, inc=1, device_id=moved(me, axis, by), device_id_type=MESH
            )
            count += 1
    pl.semaphore_wait(barrier, count)


def remote(src, dst, send, recv, target):
    return pltpu.make_async_remote_copy(
        src_ref=src, dst_ref=dst, send_sem=send, recv_sem=recv,
        device_id=target, device_id_type=MESH,
    )


def slots_kernel(src, peer, feats, tiles, out, acc):
    half = acc.shape[2] // 2
    block = acc.shape[1]

    def clear(p, _):
        acc[p] = jnp.zeros(acc.shape[1:], F32)
        return 0

    lax.fori_loop(0, acc.shape[0], clear, 0)

    def tile(t, _):
        rows = pl.ds(pl.multiple_of(src[t] * block, block), block)
        acc[peer[t]] += jnp.dot(tiles[t], feats[rows, :], preferred_element_type=F32)
        return 0

    lax.fori_loop(0, tiles.shape[0], tile, 0)

    def put(p, _):
        out[0, p] = acc[p, :, :half].astype(BF16)
        out[1, p] = acc[p, :, half:].astype(BF16)
        return 0

    lax.fori_loop(0, acc.shape[0], put, 0)


def make_slots(features, tile_vals, tile_src, tile_peer):
    block = tile_vals.shape[1]
    width = features.shape[1]
    vmem = pl.BlockSpec(memory_space=pltpu.VMEM)
    smem = pl.BlockSpec(memory_space=pltpu.SMEM)
    return pl.pallas_call(
        slots_kernel,
        out_shape=jax.ShapeDtypeStruct((2, NDOM, block, width // 2), BF16),
        in_specs=[smem, smem, vmem, vmem],
        out_specs=vmem,
        scratch_shapes=[pltpu.VMEM((NDOM, block, width), F32)],
        compiler_params=pltpu.CompilerParams(vmem_limit_bytes=VMEM_BYTES),
        name="slots",
    )(tile_src, tile_peer, features, tile_vals)


def exchange_kernel(
    slots, ib, w, agg, wg,
    xb, zr, zs, ibs,
    x_send, x_recv, x_own, z_send, z_recv, ib_send, ib_recv, ib_own,
    wa_send, wa_recv, w_own, wb_send, wb_recv, wc_send, wc_recv, wd_send, wd_recv,
):
    me = position()
    y, c, x, z = me
    block, half = xb.shape[2], xb.shape[3]
    blocks = zr.shape[2]
    rows = 32
    greet(me)

    def at_z(by):
        return lax.rem(z + (by % NZ), NZ)

    def at_x(by):
        return lax.rem(x + (by % NX), NX)

    def at_y(by):
        return lax.rem(y + (by % NY), NY)

    ib_local = pltpu.make_async_copy(ib, ibs.at[z], ib_own)
    ib_local.start()
    own_w = pltpu.make_async_copy(w.at[c, y], wg.at[c, y, x * NZ + z], w_own)
    own_w.start()

    def ib_copy(by):
        return remote(ib, ibs.at[z], ib_send.at[by - 1], ib_recv.at[by - 1], moved(me, 3, by))

    def ib_arrival(by):
        return remote(ib, ibs.at[at_z(-by)], ib_send.at[by - 1], ib_recv.at[by - 1], me)

    def wa_copy(by):
        dst = wg.at[c, y, x * NZ + z]
        return remote(w.at[c, y], dst, wa_send.at[by - 1], wa_recv.at[by - 1], moved(me, 3, by))

    def wa_arrival(by):
        dst = wg.at[c, y, x * NZ + at_z(-by)]
        return remote(w.at[c, y], dst, wa_send.at[by - 1], wa_recv.at[by - 1], me)

    def wb_ref(at):
        return wg.at[c, y, pl.ds(at * NZ, NZ)]

    def wb_copy(by):
        return remote(wb_ref(x), wb_ref(x), wb_send.at[by - 1], wb_recv.at[by - 1], moved(me, 2, by))

    def wb_arrival(by):
        dst = wb_ref(at_x(-by))
        return remote(wb_ref(x), dst, wb_send.at[by - 1], wb_recv.at[by - 1], me)

    def wc_copy(by):
        ref = wg.at[c, y]
        return remote(ref, ref, wc_send.at[by - 1], wc_recv.at[by - 1], moved(me, 0, by))

    def wc_arrival(by):
        dst = wg.at[c, at_y(-by)]
        return remote(wg.at[c, y], dst, wc_send.at[by - 1], wc_recv.at[by - 1], me)

    wd_copy = remote(wg.at[c], wg.at[c], wd_send, wd_recv, moved(me, 1, 1))
    wd_arrival = remote(wg.at[1 - c], wg.at[1 - c], wd_send, wd_recv, me)

    def x_copy(j, by):
        h, rel = ITEMS[j]
        src = slots.at[h, at_x(by) * NZ + at_z(rel)]
        return remote(src, xb.at[j, x], x_send.at[j, by - 1], x_recv.at[j, by - 1], moved(me, 2, by))

    def x_arrival(j, by):
        h, rel = ITEMS[j]
        src = slots.at[h, x * NZ + at_z(rel)]
        return remote(src, xb.at[j, at_x(-by)], x_send.at[j, by - 1], x_recv.at[j, by - 1], me)

    def x_local(j):
        h, rel = ITEMS[j]
        return pltpu.make_async_copy(slots.at[h, x * NZ + at_z(rel)], xb.at[j, x], x_own.at[j])

    def x_start(j):
        for by in (2, 1, 3):
            x_copy(j, by).start()
        x_local(j).start()

    def x_wait(j):
        x_local(j).wait()
        for by in (2, 1, 3):
            x_arrival(j, by).wait_recv()

    def z_refs(d, i):
        if i < 2:
            return xb.at[2 * i + d], zr.at[d, i, pl.ds(0, NX)]
        return zs.at[d, i - 2], zr.at[d, i]

    def z_copy(d, i):
        src, dst = z_refs(d, i)
        return remote(src, dst, z_send.at[d, i], z_recv.at[d, i], moved(me, 3, 1 - 2 * d))

    def z_arrival(d, i):
        src, dst = z_refs(d, i)
        return remote(src, dst, z_send.at[d, i], z_recv.at[d, i], me)

    def placed(at_dest, at_sender, piece, k, r):
        total = None
        for xs in range(NX):
            mine = ibs[at_dest, pl.ds(xs * NZ + at_sender, 1), :] == k
            term = jnp.where(mine, piece(xs)[pl.ds(r, rows), :].astype(F32), 0.0)
            total = term if total is None else total + term
        return total

    def each_part(body):
        def step(n, _):
            k = n // (block // rows)
            r = pl.multiple_of(lax.rem(n, block // rows) * rows, rows)
            body(k, r)
            return 0

        lax.fori_loop(0, blocks * (block // rows), step, 0)

    def combine(d, i):
        sign = 1 - 2 * d
        dest = at_z(sign * DIST[i])

        def body(k, r):
            total = placed(dest, z, lambda xs: xb.at[2 * i + d, xs], k, r)
            if i < 4:
                total += placed(dest, at_z(-sign), lambda xs: zr.at[d, i - 2, xs], k, r)
            else:
                total += zr[d, i - 2, k, pl.ds(r, rows), :].astype(F32)
            zs[d, i - 2, k, pl.ds(r, rows), :] = total.astype(BF16)

        each_part(body)

    for by in range(1, NZ):
        ib_copy(by).start()
    for j in range(4):
        x_start(j)
    own_w.wait()
    for by in range(1, NZ):
        wa_copy(by).start()
    for j in range(4, 6):
        x_start(j)
    ib_local.wait()
    for by in range(1, NZ):
        ib_arrival(by).wait_recv()

    for i in range(len(DIST)):
        for d in (0, 1):
            x_wait(2 * i + d)
            if i >= 2:
                z_arrival(d, i - 2).wait_recv()
                combine(d, i)
            if i < 2:
                z_copy(d, i).start()
        if i >= 2:
            for d in (0, 1):
                z_copy(d, i).start()
        if 2 * i + 7 < len(ITEMS):
            x_start(2 * i + 6)
            x_start(2 * i + 7)
        if i == 0:
            for by in range(1, NZ):
                wa_arrival(by).wait_recv()
            for by in range(1, NX):
                wb_copy(by).start()
        if i == 1:
            for by in range(1, NX):
                wb_arrival(by).wait_recv()
            for by in range(1, NY):
                wc_copy(by).start()
        if i == 5:
            for by in range(1, NY):
                wc_arrival(by).wait_recv()
            wd_copy.start()

    last = len(DIST)
    x_wait(2 * last)
    x_wait(2 * last + 1)
    for i in (5, 6):
        for d in (0, 1):
            z_arrival(d, i).wait_recv()

    for h in (0, 1):
        i_plus = 6 if h == 0 else 5
        i_minus = 5 if h == 0 else 6

        def body(k, r, h=h, i_plus=i_plus, i_minus=i_minus):
            total = placed(z, z, lambda xs: xb.at[2 * last + h, xs], k, r)
            total += zr[0, i_plus, k, pl.ds(r, rows), :].astype(F32)
            total += zr[1, i_minus, k, pl.ds(r, rows), :].astype(F32)
            at = pl.multiple_of(k * block + r, rows)
            agg[pl.ds(at, rows), h * half:(h + 1) * half] = total.astype(BF16)

        each_part(body)

    wd_arrival.wait_recv()
    wd_copy.wait_send()
    for by in range(1, NZ):
        ib_copy(by).wait_send()
        wa_copy(by).wait_send()
    for by in range(1, NX):
        wb_copy(by).wait_send()
    for by in range(1, NY):
        wc_copy(by).wait_send()
    for j in range(len(ITEMS)):
        for by in range(1, NX):
            x_copy(j, by).wait_send()
    for i in range(len(DIST)):
        for d in (0, 1):
            z_copy(d, i).wait_send()


def exchange(slots, ib, w):
    _, _, block, half = slots.shape
    blocks = 8
    dma = pltpu.SemaphoreType.DMA
    vmem = pl.BlockSpec(memory_space=pltpu.VMEM)
    anywhere = pl.BlockSpec(memory_space=pl.ANY)
    steps = len(DIST)
    return pl.pallas_call(
        exchange_kernel,
        out_shape=(
            jax.ShapeDtypeStruct((blocks * block, 2 * half), BF16),
            jax.ShapeDtypeStruct((NC, NY, NDOM, *w.shape[2:]), BF16),
        ),
        in_specs=[anywhere, vmem, anywhere],
        out_specs=(vmem, anywhere),
        scratch_shapes=[
            pltpu.VMEM((len(ITEMS), NX, block, half), BF16),
            pltpu.VMEM((2, steps, blocks, block, half), BF16),
            pltpu.VMEM((2, steps - 2, blocks, block, half), BF16),
            pltpu.VMEM((NZ, *ib.shape), jnp.int32),
            dma((len(ITEMS), NX - 1)),
            dma((len(ITEMS), NX - 1)),
            dma((len(ITEMS),)),
            dma((2, steps)),
            dma((2, steps)),
            dma((NZ - 1,)),
            dma((NZ - 1,)),
            dma,
            dma((NZ - 1,)),
            dma((NZ - 1,)),
            dma,
            dma((NX - 1,)),
            dma((NX - 1,)),
            dma((NY - 1,)),
            dma((NY - 1,)),
            dma,
            dma,
        ],
        compiler_params=pltpu.CompilerParams(
            collective_id=0, has_side_effects=True, vmem_limit_bytes=VMEM_BYTES
        ),
        name="exchange",
    )(slots, ib, w)


def terms_kernel(feats, agg, cot, wg, t0, t1, t2, left):
    rows = feats.shape[0]
    per = wg.shape[1]
    chunk = wg.shape[3]

    @pl.when(pl.program_id(0) == 0)
    def _():
        left[0] = feats[...].T
        left[1] = agg[...].T

    def weights(side):
        return jnp.concatenate([wg[side, n] for n in range(per)], axis=1)

    pre = jnp.dot(feats[...], weights(0), preferred_element_type=F32)
    pre += jnp.dot(agg[...], weights(1), preferred_element_type=F32)
    scale = 0.7978845608
    square = pre * pre
    t = jnp.tanh(scale * (pre + 0.044715 * (square * pre)))
    slope = 0.5 * (1.0 + t) + (0.5 * scale) * pre * (1.0 - t * t) * (1.0 + 0.134145 * square)
    grad = (cot[...].astype(F32) * slope).astype(BF16)
    for side in range(NC):
        both = jnp.dot(left[side], grad, preferred_element_type=F32)
        for n in range(per):
            v = both[:, n * chunk:(n + 1) * chunk].reshape(NX, NZ, 3, 8, chunk)
            for xs in range(NX):
                t0[side, n, :, xs] = v[xs, :, 0].astype(BF16)
                t1[side, :, n, xs] = v[xs, :, 1].astype(BF16)
                t2[side, xs, :, n] = v[xs, :, 2].astype(BF16)


def make_terms(features, agg, cotangent, wg):
    rows, width = features.shape
    chunk = wg.shape[3]
    per = 2
    whole = pl.BlockSpec((rows, width), lambda q: (0, 0))
    tile = (8, chunk)
    return pl.pallas_call(
        terms_kernel,
        grid=(NY // per,),
        out_shape=(
            jax.ShapeDtypeStruct((NC, NY, NZ, NX, *tile), BF16),
            jax.ShapeDtypeStruct((NC, NZ, NY, NX, *tile), BF16),
            jax.ShapeDtypeStruct((NC, NX, NZ, NY, *tile), BF16),
        ),
        in_specs=[
            whole,
            whole,
            pl.BlockSpec((rows, per * chunk), lambda q: (0, q)),
            pl.BlockSpec((NC, per, width, chunk), lambda q: (0, q, 0, 0)),
        ],
        out_specs=(
            pl.BlockSpec((NC, per, NZ, NX, *tile), lambda q: (0, q, 0, 0, 0, 0)),
            pl.BlockSpec((NC, NZ, per, NX, *tile), lambda q: (0, 0, q, 0, 0, 0)),
            pl.BlockSpec((NC, NX, NZ, per, *tile), lambda q: (0, 0, 0, q, 0, 0)),
        ),
        scratch_shapes=[pltpu.VMEM((2, width, rows), BF16)],
        compiler_params=pltpu.CompilerParams(vmem_limit_bytes=VMEM_BYTES),
        name="terms",
    )(features, agg, cotangent, wg)


ORDER = ((0, 3, 2), (3, 0, 2), (2, 3, 0))


def reduce_kernel(
    t0, t1, t2, out_self, out_neigh,
    own0, own1, own2, got0, got1, got2, mid0, mid1, mid2, low0, low1, low2,
    a0, a1, a2, b0, b1, b2, d0, d1, d2, every,
    own_sem, c_send, c_recv, s_send, s_recv, g_send, g_recv, p_send, p_recv,
):
    me = position()
    y, c = me[0], me[1]
    given = (t0, t1, t2)
    got = (got0, got1, got2)
    parts = ((own0, own1, own2), (mid0, mid1, mid2), (low0, low1, low2))
    inbox = ((a0, a1, a2), (b0, b1, b2), (d0, d1, d2))
    own = parts[0]
    greet(me)

    def load(j):
        return pltpu.make_async_copy(given[j].at[c], own[j], own_sem.at[j])

    def to_partner(j, target):
        return remote(given[j].at[1 - c], got[j], c_send.at[j], c_recv.at[j], target)

    for j in range(3):
        to_partner(j, moved(me, 1, 1)).start()
        load(j).start()

    def hop(j, s, by, arriving=False):
        axis = ORDER[j][s]
        size = SIZES[axis]
        here = me[axis]
        src = parts[s][j].at[lax.rem(here + by, size)]
        send, recv = s_send.at[s, j, by - 1], s_recv.at[s, j, by - 1]
        if arriving:
            return remote(src, inbox[s][j].at[lax.rem(here + size - by, size)], send, recv, me)
        return remote(src, inbox[s][j].at[here], send, recv, moved(me, axis, by))

    def hops(j, s):
        return range(1, SIZES[ORDER[j][s]])

    for j in range(3):
        load(j).wait()
        to_partner(j, me).wait_recv()
        n1, n2 = own[j].shape[:2]

        def add(n, _, j=j, n2=n2):
            a, b = n // n2, lax.rem(n, n2)
            own[j][a, b] = (own[j][a, b].astype(F32) + got[j][a, b].astype(F32)).astype(BF16)
            return 0

        lax.fori_loop(0, n1 * n2, add, 0)
        for by in hops(j, 0):
            hop(j, 0, by).start()

    for s in range(3):
        for j in range(3):
            axis = ORDER[j][s]
            size = SIZES[axis]
            here = me[axis]
            for by in hops(j, s):
                hop(j, s, by, arriving=True).wait_recv()

            def total(at, j=j, s=s, here=here, size=size):
                out = parts[s][j][(here, *at)].astype(F32)
                for by in range(1, size):
                    out += inbox[s][j][(lax.rem(here + by, size), *at)].astype(F32)
                return out

            if s == 2:
                every[c, y, j] = total(())
                continue

            def add(n, _, j=j, s=s, total=total):
                parts[s + 1][j][n] = total((n,)).astype(BF16)
                return 0

            lax.fori_loop(0, parts[s + 1][j].shape[0], add, 0)
            for by in hops(j, s + 1):
                hop(j, s + 1, by).start()

    def gather(by, arriving=False):
        dst = every.at[c, lax.rem(y + NY - by, NY) if arriving else y]
        target = me if arriving else moved(me, 0, by)
        return remote(every.at[c, y], dst, g_send.at[by - 1], g_recv.at[by - 1], target)

    for by in range(1, NY):
        gather(by).start()
    for by in range(1, NY):
        gather(by, arriving=True).wait_recv()
    pair = remote(every.at[c], every.at[c], p_send, p_recv, moved(me, 1, 1))
    pair.start()
    remote(every.at[c], every.at[1 - c], p_send, p_recv, me).wait_recv()
    for side, out in ((0, out_self), (1, out_neigh)):
        for n in range(NY):
            for j in range(3):
                out[j * 8:(j + 1) * 8, n * 128:(n + 1) * 128] = every[side, n, j]
    pair.wait_send()
    for by in range(1, NY):
        gather(by).wait_send()
    for j in range(3):
        to_partner(j, moved(me, 1, 1)).wait_send()
        for s in range(3):
            for by in hops(j, s):
                hop(j, s, by).wait_send()


def reduce_terms(terms):
    dma = pltpu.SemaphoreType.DMA
    shapes = [t.shape[1:] for t in terms]
    tile = shapes[0][-2:]
    vmem = pl.BlockSpec(memory_space=pltpu.VMEM)
    scratch = [pltpu.VMEM(s[skip:], BF16) for skip in (0, 0, 1, 2) for s in shapes]
    scratch += [pltpu.VMEM(s[skip:], BF16) for skip in (0, 1, 2) for s in shapes]
    out = jax.ShapeDtypeStruct((3 * tile[0], NY * tile[1]), F32)
    return pl.pallas_call(
        reduce_kernel,
        out_shape=(out, out),
        in_specs=[pl.BlockSpec(memory_space=pl.ANY)] * 3,
        out_specs=(vmem, vmem),
        scratch_shapes=scratch
        + [
            pltpu.VMEM((NC, NY, 3, *tile), F32),
            dma((3,)),
            dma((3,)),
            dma((3,)),
            dma((3, 3, 7)),
            dma((3, 3, 7)),
            dma((NY - 1,)),
            dma((NY - 1,)),
            dma,
            dma,
        ],
        compiler_params=pltpu.CompilerParams(
            collective_id=1, has_side_effects=True, vmem_limit_bytes=VMEM_BYTES
        ),
        name="reduce",
    )(*terms)


def shards(features, cotangent, w_self, w_neigh, tile_vals, tile_src, tile_peer, in_block):
    half = features.shape[1] // 2
    own_rows, hidden = w_self.shape
    chunk = hidden // NY
    w = jnp.stack([w_self, w_neigh]).reshape(NC, own_rows, NY, chunk).transpose(0, 2, 1, 3)
    ib = jnp.broadcast_to(in_block[:, None], (NDOM, half))
    slots = make_slots(features, tile_vals, tile_src, tile_peer)
    agg, wg = exchange(slots, ib, w)
    wg = wg.reshape(NC, NY, NDOM * own_rows, chunk)
    terms = make_terms(features, agg, cotangent, wg)
    return reduce_terms(terms)


def solution(mesh):
    split = Mesh(mesh.devices.reshape(SIZES), AXES)
    every = P(AXES)
    rows = P(AXES, None)
    placed = (
        rows,
        rows,
        P(("x", "z"), None),
        P(("x", "z"), None),
        P(AXES, None, None),
        every,
        every,
        every,
    )
    out = P(("x", "z"), None)
    return jax.shard_map(
        shards, mesh=split, in_specs=placed, out_specs=(out, out), check_vma=False
    )
```

time: 387 us -> 231 us (0.60)
  waiting for transfers between devices: 283 us -> 0 us
  Pallas kernels: 0 us -> 223 us
  matrix products: 37 us -> 0 us
  local copies, waits for them, and re-layouts: 32.9 us -> 6.06 us
  starting transfers between devices: 14.3 us -> 0 us
  between operations: 13.9 us -> 0.65 us
  other arithmetic: 4.99 us -> 0.65 us
    pallas_call x0 -> x4, Pallas kernels: none -> 223 us  [the longest x1 148 us: exchange(): pl.pallas_call(exchange_kernel, out_shape=(jax.ShapeDtypeStruct((blocks *...]
    all_to_all x1 -> x0, waiting for transfers between devices: 152 us -> none  [shards(): lax.all_to_all(slots, DOM, split_axis=0, concat_axis=0, tiled=True)]
    all_gather x2 -> x0, waiting for transfers between devices: 46.7 us -> none  [the longest x1 46.7 us: over_pieces(): return lax.all_gather(x, axis).astype(jnp.float32).sum(0)]
    unnamed x5 -> x0, waiting for transfers between devices: 44.7 us -> none
    reduce_scatter x1 -> x0, waiting for transfers between devices: 39.5 us -> none  [own_rows(): total = lax.psum_scatter(total, axis, scatter_dimension=0, tiled=True)]
    dot_general x7 -> x0, matrix products: 37 us -> none  [the longest x1 9.18 us: shards(): jnp.einsum('tij,tjf->tif', tile_vals, picked, preferred_element_type=jnp....]
    all_to_all x1 -> x0, starting transfers between devices: 13.9 us -> none  [shards(): lax.all_to_all(slots, DOM, split_axis=0, concat_axis=0, tiled=True)]
    dot_general x1 -> x0, local copies, waits for them, and re-layouts: 12.9 us -> none  [shards(): jnp.einsum('tij,tjf->tif', tile_vals, picked, preferred_element_type=jnp....]
  transfers between devices with their start and end apart: 5 -> 0, of which waited for: 4 -> 0; matrix products, arithmetic and copies ran while one was open for 3% -> 0% of each run, Pallas kernels for 0% -> 0%
where the time goes in v1:
time: 231 us
  Pallas kernels  223 us (97%)
  local copies, waits for them, and re-layouts  6.06 us (3%)
    pallas_call x1, Pallas kernels, exchange(): pl.pallas_call(exchange_kernel, out_shape=(jax.ShapeDtypeStruct((blocks *...  148 us
    pallas_call x1, Pallas kernels, reduce_terms(): pl.pallas_call(reduce_kernel, out_shape=(out, out), in_specs=[pl.BlockSpe...  44 us
    pallas_call x1, Pallas kernels, make_terms(): pl.pallas_call(terms_kernel, grid=(NY // per,), out_shape=(jax.ShapeDtype...  18.7 us
    pallas_call x1, Pallas kernels, make_slots(): pl.pallas_call(slots_kernel, out_shape=jax.ShapeDtypeStruct((2, NDOM, blo...  12.5 us
    unnamed x4, local copies, waits for them, and re-layouts  4.7 us

profile of v1, /device:TPU:1, one launch (start us, length us, event | category | flops | bytes accessed | tf_op | source)
XLA Modules:
  0.0 230.7 jit_solution(16545939726617435292)
XLA Ops:
  0.6 0.8 copy.12
  1.4 0.8 copy.13
  2.3 0.7 maximum_bitcast_fusion.w
  2.9 1.3 broadcast_in_dim.2.ib
  4.3 12.5 %slots.1 = bf16[2,32,128,384]{3,2,1,0:T(8,128)(2,1)} custom-call(s32[32]{0:T(128)} %src.1, s32[32]{0:T(128)} %peer.1, bf16[1024,768]{1,0:T(8,128)(2,1)} %feats.3, bf16[32,128,128]{2,1,0:T(8,128)(2,1)} %tiles.1), custom_call_target="tpu_custom_call" | custom-call | tf_op jit(solution)/shard_map/slots/pallas_call | solution.py:87
  16.8 148.1 %exchange.1 = (bf16[1024,768]{1,0:T(8,128)(2,1)}, bf16[2,8,32,24,128]{4,3,2,1,0:T(8,128)(2,1)}) custom-call(bf16[2,32,128,384]{3,2,1,0:T(8,128)(2,1)} %slots.1, s32[32,384]{1,0:T(8,128)} %broadcast_in_dim.2.ib, bf16[2,8,24,128]{3,2,1,0:T(8,128)(2,1)} %maximum_bitcast_fusion.w), custom_call_target="tpu_custom_call" | custom-call | tf_op jit(solution)/shard_map/exchange/pallas_call | solution.py:314
  164.9 18.7 %terms.1 = (bf16[2,8,8,4,8,128]{5,4,3,2,1,0:T(8,128)(2,1)}, bf16[2,8,8,4,8,128]{5,4,3,2,1,0:T(8,128)(2,1)}, bf16[2,4,8,8,8,128]{5,4,3,2,1,0:T(8,128)(2,1)}) custom-call(bf16[1024,768]{1,0:T(8,128)(2,1)} %feats.3, bf16[1024,768]{1,0:T(8,128)(2,1)} %get-tuple-element.7.agg, bf16[1024,1024]{1,0:T(8,128)(2,1)} %cot.1, bf16[2,8,768,128]{3,2,1,0:T(8,128)(2,1)} %bitcast.9), custom_call_target="tpu_custom_call" | custom-call | tf_op jit(solution)/shard_map/terms/pallas_call | solution.py:388
  183.6 44.0 %reduce.1 = (f32[24,1024]{1,0:T(8,128)}, f32[24,1024]{1,0:T(8,128)}) custom-call(bf16[2,8,8,4,8,128]{5,4,3,2,1,0:T(8,128)(2,1)} %get-tuple-element.9.t0, bf16[2,8,8,4,8,128]{5,4,3,2,1,0:T(8,128)(2,1)} %get-tuple-element.10.t1, bf16[2,4,8,8,8,128]{5,4,3,2,1,0:T(8,128)(2,1)} %get-tuple-element.11.t2), custom_call_target="tpu_custom_call" | custom-call | tf_op jit(solution)/shard_map/reduce/pallas_call | solution.py:528
  227.6 1.5 copy.16
  229.2 1.5 copy.17
  (2 shorter events, 0.0 us)

commit v2 on v0

v2 whole, which is shorter than its diff:
```python
import functools

import jax
import jax.numpy as jnp
from jax import lax
from jax.experimental import pallas as pl
from jax.experimental.pallas import tpu as pltpu
from jax.sharding import Mesh
from jax.sharding import PartitionSpec as P

AXES = ("y", "c", "x", "z")
SIZES = (8, 2, 4, 8)
NY, NC, NX, NZ = SIZES
NDOM = NX * NZ
MESH = pl.DeviceIdType.MESH
VMEM_BYTES = 67043328
F32 = jnp.float32
BF16 = jnp.bfloat16

DIST = (4, 3, 3, 2, 2, 1, 1)
ITEMS = []
for _i, _d in enumerate(DIST):
    ITEMS += [(_i % 2, _d), (1 - _i % 2, -_d)]
ITEMS += [(0, 0), (1, 0)]


def position():
    return tuple(lax.axis_index(a) for a in AXES)


def moved(me, axis, by):
    return tuple(
        lax.rem(m + (by % SIZES[axis]), SIZES[axis]) if a == axis else m
        for a, m in enumerate(me)
    )


def greet(me):
    barrier = pltpu.get_barrier_semaphore()
    count = 0
    for axis, size in enumerate(SIZES):
        for by in range(1, size):
            pl.semaphore_signal(
                barrier, inc=1, device_id=moved(me, axis, by), device_id_type=MESH
            )
            count += 1
    pl.semaphore_wait(barrier, count)


def remote(src, dst, send, recv, target):
    return pltpu.make_async_remote_copy(
        src_ref=src, dst_ref=dst, send_sem=send, recv_sem=recv,
        device_id=target, device_id_type=MESH,
    )


ORDER = ((0, 3, 2), (3, 0, 2), (2, 3, 0))


def step_kernel(
    idx, inb, tiles, feats, cot_in, w_self, w_neigh, out, wg,
    ct, sl, xb, zr, zs, ibs, cot, w, pre_own, agg, left, grad,
    out0, out1, out2, own0, own1, own2, got0, got1, got2, mid0, mid1, mid2, low0, low1, low2,
    a0, a1, a2, b0, b1, b2, d0, d1, d2, every,
    x_send, x_recv, z_send, z_recv, ib_send, ib_recv, cot_sem, w_sem,
    wa_send, wa_recv, w_own, wb_send, wb_recv, wc_send, wc_recv, wd_send, wd_recv,
    c_send, c_recv, s_send, s_recv, g_send, g_recv, p_send, p_recv,
):
    me = position()
    y, c, x, z = me
    block, half = xb.shape[2], xb.shape[3]
    blocks = zr.shape[2]
    owned = w_self.shape[0]
    chunk = wg.shape[3]
    count = tiles.shape[0]
    rows = 32
    last = len(DIST)
    final = last - 1
    groups = z_send.shape[1] - final
    per = blocks // groups

    def at_z(by):
        return lax.rem(z + (by % NZ), NZ)

    def at_x(by):
        return lax.rem(x + (by % NX), NX)

    def at_y(by):
        return lax.rem(y + (by % NY), NY)

    for s in range(NDOM):
        ibs[z, s:s + 1, :] = jnp.full((1, half), inb[s], jnp.int32)
    load_cot = pltpu.make_async_copy(cot_in, cot, cot_sem)
    load_cot.start()
    ct[...] = jnp.zeros_like(ct)

    def chain(t, _):
        ct[t] = tiles[t].astype(F32) + ct[idx[t]]
        return 0

    lax.fori_loop(0, count, chain, 0)

    def slots(rel):
        j0, j1 = (
            next(j for j, (h, at) in enumerate(ITEMS) if h == side and (at - rel) % NZ == 0)
            for side in (0, 1)
        )

        def one(by, _):
            p = lax.rem(x + by, NX) * NZ + at_z(rel)
            parts = [ct[idx[count + p * blocks + b]].astype(BF16) for b in range(blocks)]
            value = jnp.dot(jnp.concatenate(parts, axis=1), feats[...], preferred_element_type=F32)
            sl[j0, by] = value[:, :half].astype(BF16)
            sl[j1, by] = value[:, half:].astype(BF16)
            return 0

        lax.fori_loop(0, NX, one, 0)
        xb[j0, x] = sl[j0, 0]
        xb[j1, x] = sl[j1, 0]

    slots(4)
    greet(me)

    def ib_copy(by):
        ref = ibs.at[z]
        return remote(ref, ref, ib_send.at[by - 1], ib_recv.at[by - 1], moved(me, 3, by))

    def ib_arrival(by):
        return remote(ibs.at[z], ibs.at[at_z(-by)], ib_send.at[by - 1], ib_recv.at[by - 1], me)

    def wg_rows(at, size):
        return wg.at[c, y, pl.ds(pl.multiple_of(at * owned, owned), size * owned)]

    def w_src(ref):
        return ref.at[:, pl.ds(pl.multiple_of(y * chunk, chunk), chunk)]

    def w_local(ref):
        return pltpu.make_async_copy(w_src(ref), wg_rows(x * NZ + z, 1), w_own)

    def wa_copy(ref, by):
        dst = wg_rows(x * NZ + z, 1)
        return remote(w_src(ref), dst, wa_send.at[by - 1], wa_recv.at[by - 1], moved(me, 3, by))

    def wa_arrival(by):
        dst = wg_rows(x * NZ + at_z(-by), 1)
        return remote(w_src(w_self), dst, wa_send.at[by - 1], wa_recv.at[by - 1], me)

    def wb_copy(by):
        ref = wg_rows(x * NZ, NZ)
        return remote(ref, ref, wb_send.at[by - 1], wb_recv.at[by - 1], moved(me, 2, by))

    def wb_arrival(by):
        dst = wg_rows(at_x(-by) * NZ, NZ)
        return remote(wg_rows(x * NZ, NZ), dst, wb_send.at[by - 1], wb_recv.at[by - 1], me)

    def wc_copy(by):
        ref = wg.at[c, y]
        return remote(ref, ref, wc_send.at[by - 1], wc_recv.at[by - 1], moved(me, 0, by))

    def wc_arrival(by):
        dst = wg.at[c, at_y(-by)]
        return remote(wg.at[c, y], dst, wc_send.at[by - 1], wc_recv.at[by - 1], me)

    wd_copy = remote(wg.at[c], wg.at[c], wd_send, wd_recv, moved(me, 1, 1))
    wd_arrival = remote(wg.at[1 - c], wg.at[1 - c], wd_send, wd_recv, me)
    load_w = pltpu.make_async_copy(wg, w, w_sem)

    def x_copy(j, by, arriving=False):
        send, recv = x_send.at[j, by - 1], x_recv.at[j, by - 1]
        if arriving:
            return remote(sl.at[j, by], xb.at[j, at_x(-by)], send, recv, me)
        return remote(sl.at[j, by], xb.at[j, x], send, recv, moved(me, 2, by))

    def x_start(j):
        for by in (2, 1, 3):
            x_copy(j, by).start()

    def x_wait(j):
        for by in (2, 1, 3):
            x_copy(j, by, arriving=True).wait_recv()

    def z_copy(d, i, g=0, arriving=False):
        if i < 2:
            src, dst = xb.at[2 * i + d], zr.at[d, i, pl.ds(0, NX)]
        elif i < final:
            src, dst = zs.at[d, i - 2], zr.at[d, i]
        else:
            piece = pl.ds(g * per, per)
            src, dst = zs.at[d, i - 2, piece], zr.at[d, i, piece]
        target = me if arriving else moved(me, 3, 1 - 2 * d)
        return remote(src, dst, z_send.at[d, i + g], z_recv.at[d, i + g], target)

    def pieces(i):
        return range(groups if i == final else 1)

    def placed(at_dest, at_sender, piece, k, r):
        total = None
        for xs in range(NX):
            mine = ibs[at_dest, pl.ds(xs * NZ + at_sender, 1), :] == k
            term = jnp.where(mine, piece(xs)[pl.ds(r, rows), :].astype(F32), 0.0)
            total = term if total is None else total + term
        return total

    def each_part(first, number, body):
        def step(n, _):
            k = first + n // (block // rows)
            r = pl.multiple_of(lax.rem(n, block // rows) * rows, rows)
            body(k, r)
            return 0

        lax.fori_loop(0, number * (block // rows), step, 0)

    def combine(d, i):
        sign = 1 - 2 * d
        dest = at_z(sign * DIST[i])

        def body(k, r):
            total = placed(dest, z, lambda xs: xb.at[2 * i + d, xs], k, r)
            if i < 4:
                total += placed(dest, at_z(-sign), lambda xs: zr.at[d, i - 2, xs], k, r)
            else:
                total += zr[d, i - 2, k, pl.ds(r, rows), :].astype(F32)
            zs[d, i - 2, k, pl.ds(r, rows), :] = total.astype(BF16)

        each_part(0, blocks, body)

    def transpose_feats():
        def one(n, _):
            at = pl.ds(pl.multiple_of(n * block, block), block)
            left[0, :, at] = feats[at, :].T
            return 0

        lax.fori_loop(0, blocks, one, 0)

    def own_product():
        def one(n, _):
            both = jnp.concatenate([w[0, 2 * n], w[0, 2 * n + 1]], axis=1)
            value = jnp.dot(feats[...], both, preferred_element_type=F32)
            pre_own[n] = value
            return 0

        lax.fori_loop(0, NY // 2, one, 0)

    for j in range(2):
        x_start(j)
    for by in range(1, NZ):
        ib_copy(by).start()
    for side, ref in ((0, w_self), (1, w_neigh)):

        @pl.when(c == side)
        def _(ref=ref):
            w_local(ref).start()
            for by in range(1, NZ):
                wa_copy(ref, by).start()

    slots(3)
    slots(-3)
    for j in range(2, 4):
        x_start(j)

    for i in range(last):
        for d in (0, 1):
            x_wait(2 * i + d)
            if i >= 2:
                z_copy(d, i - 2, arriving=True).wait_recv()
                combine(d, i)
            if i < 2:
                z_copy(d, i).start()
        if i >= 2:
            for g in pieces(i):
                for d in (0, 1):
                    z_copy(d, i, g).start()
        if 2 * i + 5 < len(ITEMS):
            x_start(2 * i + 4)
            x_start(2 * i + 5)
        if i == 0:
            slots(2)
            slots(-2)
            w_local(w_self).wait()
            for by in range(1, NZ):
                wa_copy(w_self, by).wait_send()
                wa_arrival(by).wait_recv()
            for by in range(1, NX):
                wb_copy(by).start()
            for by in range(1, NZ):
                ib_arrival(by).wait_recv()
        if i == 1:
            slots(1)
            slots(-1)
            slots(0)
            for by in range(1, NX):
                wb_arrival(by).wait_recv()
            for by in range(1, NY):
                wc_copy(by).start()
        if i == 2:
            transpose_feats()
        if i == 4:
            for by in range(1, NY):
                wc_arrival(by).wait_recv()
            wd_copy.start()
        if i == 5:
            wd_arrival.wait_recv()
            load_w.start()
            load_w.wait()
            own_product()

    load_cot.wait()
    x_wait(2 * last)
    x_wait(2 * last + 1)
    for d in (0, 1):
        z_copy(d, final - 1, arriving=True).wait_recv()

    span = per * block
    scale = 0.7978845608
    for g in range(groups):
        for d in (0, 1):
            z_copy(d, final, g, arriving=True).wait_recv()
        for h in (0, 1):

            def body(k, r, h=h):
                total = placed(z, z, lambda xs: xb.at[2 * last + h, xs], k, r)
                total += zr[h, final, k, pl.ds(r, rows), :].astype(F32)
                total += zr[1 - h, final - 1, k, pl.ds(r, rows), :].astype(F32)
                at = pl.multiple_of((k - g * per) * block + r, rows)
                agg[pl.ds(at, rows), h * half:(h + 1) * half] = total.astype(BF16)

            each_part(g * per, per, body)
        here = pl.ds(g * span, span)
        left[1, :, here] = agg[...].T

        def gradient(n, _, here=here):
            both = jnp.concatenate([w[1, 2 * n], w[1, 2 * n + 1]], axis=1)
            pre = pre_own[n, here, :]
            pre += jnp.dot(agg[...], both, preferred_element_type=F32)
            square = pre * pre
            t = jnp.tanh(scale * (pre + 0.044715 * (square * pre)))
            slope = 0.5 * (1.0 + t)
            slope += (0.5 * scale) * pre * (1.0 - t * t) * (1.0 + 0.134145 * square)
            columns = pl.ds(pl.multiple_of(n * 2 * chunk, 2 * chunk), 2 * chunk)
            grad[n, here, :] = (cot[here, columns].astype(F32) * slope).astype(BF16)
            return 0

        lax.fori_loop(0, NY // 2, gradient, 0)

    own = (own0, own1, own2)
    outgoing = (out0, out1, out2)
    got = (got0, got1, got2)
    parts = (own, (mid0, mid1, mid2), (low0, low1, low2))
    inbox = ((a0, a1, a2), (b0, b1, b2), (d0, d1, d2))

    def terms(side, n, to):
        both = jnp.dot(left[side], grad[n], preferred_element_type=F32)
        for e in range(2):
            v = both[:, e * chunk:(e + 1) * chunk].reshape(NX, NZ, 3, 8, chunk)
            for xs in range(NX):
                to[0][2 * n + e, :, xs] = v[xs, :, 0].astype(BF16)
                to[1][:, 2 * n + e, xs] = v[xs, :, 1].astype(BF16)
                to[2][xs, :, 2 * n + e] = v[xs, :, 2].astype(BF16)

    def to_partner(j, n, target):
        at = pl.ds(2 * n, 2)
        if j == 0:
            src, dst = out0.at[at], got0.at[at]
        elif j == 1:
            src, dst = out1.at[:, at], got1.at[:, at]
        else:
            src, dst = out2.at[:, :, at], got2.at[:, :, at]
        return remote(src, dst, c_send.at[j, n], c_recv.at[j, n], target)

    for n in range(NY // 2):
        terms(1 - c, n, outgoing)
        for j in range(3):
            to_partner(j, n, moved(me, 1, 1)).start()

    def own_terms(n, _):
        terms(c, n, own)
        return 0

    lax.fori_loop(0, NY // 2, own_terms, 0)

    def hop(j, s, by, arriving=False):
        axis = ORDER[j][s]
        size = SIZES[axis]
        at = me[axis]
        src = parts[s][j].at[lax.rem(at + by, size)]
        send, recv = s_send.at[s, j, by - 1], s_recv.at[s, j, by - 1]
        if arriving:
            return remote(src, inbox[s][j].at[lax.rem(at + size - by, size)], send, recv, me)
        return remote(src, inbox[s][j].at[at], send, recv, moved(me, axis, by))

    def hops(j, s):
        return range(1, SIZES[ORDER[j][s]])

    for j in range(3):
        for n in range(NY // 2):
            to_partner(j, n, me).wait_recv()
        n1, n2 = own[j].shape[:2]

        def add(n, _, j=j, n2=n2):
            a, b = n // n2, lax.rem(n, n2)
            own[j][a, b] = (own[j][a, b].astype(F32) + got[j][a, b].astype(F32)).astype(BF16)
            return 0

        lax.fori_loop(0, n1 * n2, add, 0)
        for by in hops(j, 0):
            hop(j, 0, by).start()

    for s in range(3):
        for j in range(3):
            axis = ORDER[j][s]
            size = SIZES[axis]
            at_axis = me[axis]
            for by in hops(j, s):
                hop(j, s, by, arriving=True).wait_recv()

            def total(at, j=j, s=s, at_axis=at_axis, size=size):
                value = parts[s][j][(at_axis, *at)].astype(F32)
                for by in range(1, size):
                    value += inbox[s][j][(lax.rem(at_axis + by, size), *at)].astype(F32)
                return value

            if s == 2:
                every[c, y, j] = total(()).astype(BF16)
                continue

            def add(n, _, j=j, s=s, total=total):
                parts[s + 1][j][n] = total((n,)).astype(BF16)
                return 0

            lax.fori_loop(0, parts[s + 1][j].shape[0], add, 0)
            for by in hops(j, s + 1):
                hop(j, s + 1, by).start()

    def gather(by, arriving=False):
        dst = every.at[c, at_y(-by) if arriving else y]
        target = me if arriving else moved(me, 0, by)
        return remote(every.at[c, y], dst, g_send.at[by - 1], g_recv.at[by - 1], target)

    for by in range(1, NY):
        gather(by).start()
    for by in range(1, NY):
        gather(by, arriving=True).wait_recv()
    pair = remote(every.at[c], every.at[c], p_send, p_recv, moved(me, 1, 1))
    pair.start()
    remote(every.at[c], every.at[1 - c], p_send, p_recv, me).wait_recv()
    for side in (0, 1):
        for n in range(NY):
            for j in range(3):
                out[side, j * 8:(j + 1) * 8, n * chunk:(n + 1) * chunk] = every[side, n, j].astype(F32)

    pair.wait_send()
    wd_copy.wait_send()
    for by in range(1, NZ):
        ib_copy(by).wait_send()
    for by in range(1, NX):
        wb_copy(by).wait_send()
    for by in range(1, NY):
        wc_copy(by).wait_send()
        gather(by).wait_send()
    for j in range(len(ITEMS)):
        for by in range(1, NX):
            x_copy(j, by).wait_send()
    for i in range(last):
        for d in (0, 1):
            for g in pieces(i):
                z_copy(d, i, g).wait_send()
    for j in range(3):
        for n in range(NY // 2):
            to_partner(j, n, moved(me, 1, 1)).wait_send()
        for s in range(3):
            for by in hops(j, s):
                hop(j, s, by).wait_send()


def shards(features, cotangent, w_self, w_neigh, tile_vals, tile_src, tile_peer, in_block):
    count, block, _ = tile_vals.shape
    nodes, width = features.shape
    half = width // 2
    owned, hidden = w_self.shape
    blocks = nodes // block
    chunk = hidden // NY

    key = tile_peer * blocks + tile_src
    order = jnp.arange(count, dtype=jnp.int32)
    wanted = jnp.concatenate([key, jnp.arange(NDOM * blocks, dtype=jnp.int32)])
    limit = jnp.concatenate([order, jnp.full((NDOM * blocks,), count, jnp.int32)])
    found = (wanted[:, None] == key[None, :]) & (order[None, :] < limit[:, None])
    idx = jnp.max(jnp.where(found, order[None, :], -1), axis=1)
    idx = jnp.where(idx < 0, count, idx)

    dma = pltpu.SemaphoreType.DMA
    vmem = pl.BlockSpec(memory_space=pltpu.VMEM)
    smem = pl.BlockSpec(memory_space=pltpu.SMEM)
    anywhere = pl.BlockSpec(memory_space=pl.ANY)
    steps = len(DIST)
    items = len(ITEMS)
    groups = 4
    thirds = [(NY, NZ, NX, 8, chunk), (NZ, NY, NX, 8, chunk), (NX, NZ, NY, 8, chunk)]
    scratch = [
        pltpu.VMEM((count + 1, block, block), F32),
        pltpu.VMEM((items, NX, block, half), BF16),
        pltpu.VMEM((items, NX, block, half), BF16),
        pltpu.VMEM((2, steps, blocks, block, half), BF16),
        pltpu.VMEM((2, steps - 2, blocks, block, half), BF16),
        pltpu.VMEM((NZ, NDOM, half), jnp.int32),
        pltpu.VMEM((nodes, hidden), BF16),
        pltpu.VMEM((NC, NY, width, chunk), BF16),
        pltpu.VMEM((NY // 2, nodes, 2 * chunk), F32),
        pltpu.VMEM((nodes // groups, width), BF16),
        pltpu.VMEM((2, width, nodes), BF16),
        pltpu.VMEM((NY // 2, nodes, 2 * chunk), BF16),
    ]
    for skip in (0, 0, 0, 1, 2, 0, 1, 2):
        scratch += [pltpu.VMEM(t[skip:], BF16) for t in thirds]
    scratch += [
        pltpu.VMEM((NC, NY, 3, 8, chunk), BF16),
        dma((items, NX - 1)),
        dma((items, NX - 1)),
        dma((2, steps - 1 + groups)),
        dma((2, steps - 1 + groups)),
        dma((NZ - 1,)),
        dma((NZ - 1,)),
        dma,
        dma,
        dma((NZ - 1,)),
        dma((NZ - 1,)),
        dma,
        dma((NX - 1,)),
        dma((NX - 1,)),
        dma((NY - 1,)),
        dma((NY - 1,)),
        dma,
        dma,
        dma((3, NY // 2)),
        dma((3, NY // 2)),
        dma((3, 3, 7)),
        dma((3, 3, 7)),
        dma((NY - 1,)),
        dma((NY - 1,)),
        dma,
        dma,
    ]
    out, _ = pl.pallas_call(
        step_kernel,
        out_shape=(
            jax.ShapeDtypeStruct((NC, owned, hidden), F32),
            jax.ShapeDtypeStruct((NC, NY, width, chunk), BF16),
        ),
        in_specs=[smem, smem, vmem, vmem, anywhere, anywhere, anywhere],
        out_specs=(vmem, anywhere),
        scratch_shapes=scratch,
        compiler_params=pltpu.CompilerParams(
            collective_id=0, has_side_effects=True, vmem_limit_bytes=VMEM_BYTES
        ),
        name="step",
    )(idx, in_block, tile_vals, features, cotangent, w_self, w_neigh)
    return out[0], out[1]


def solution(mesh):
    split = Mesh(mesh.devices.reshape(SIZES), AXES)
    every = P(AXES)
    rows = P(AXES, None)
    placed = (
        rows,
        rows,
        P(("x", "z"), None),
        P(("x", "z"), None),
        P(AXES, None, None),
        every,
        every,
        every,
    )
    out = P(("x", "z"), None)
    return jax.shard_map(
        shards, mesh=split, in_specs=placed, out_specs=(out, out), check_vma=False
    )
```

time: 387 us -> 189 us (0.49)
  waiting for transfers between devices: 283 us -> 0 us
  Pallas kernels: 0 us -> 185 us
  matrix products: 37 us -> 0 us
  local copies, waits for them, and re-layouts: 32.9 us -> 1.63 us
  starting transfers between devices: 14.3 us -> 0 us
  between operations: 13.9 us -> 0.64 us
    pallas_call x0 -> x1, Pallas kernels: none -> 185 us  [shards(): pl.pallas_call(step_kernel, out_shape=(jax.ShapeDtypeStruct((NC, owned, h...]
    all_to_all x1 -> x0, waiting for transfers between devices: 152 us -> none  [shards(): lax.all_to_all(slots, DOM, split_axis=0, concat_axis=0, tiled=True)]
    all_gather x2 -> x0, waiting for transfers between devices: 46.7 us -> none  [the longest x1 46.7 us: over_pieces(): return lax.all_gather(x, axis).astype(jnp.float32).sum(0)]
    unnamed x5 -> x0, waiting for transfers between devices: 44.7 us -> none
    reduce_scatter x1 -> x0, waiting for transfers between devices: 39.5 us -> none  [own_rows(): total = lax.psum_scatter(total, axis, scatter_dimension=0, tiled=True)]
    dot_general x7 -> x0, matrix products: 37 us -> none  [the longest x1 9.18 us: shards(): jnp.einsum('tij,tjf->tif', tile_vals, picked, preferred_element_type=jnp....]
    all_to_all x1 -> x0, starting transfers between devices: 13.9 us -> none  [shards(): lax.all_to_all(slots, DOM, split_axis=0, concat_axis=0, tiled=True)]
    dot_general x1 -> x0, local copies, waits for them, and re-layouts: 12.9 us -> none  [shards(): jnp.einsum('tij,tjf->tif', tile_vals, picked, preferred_element_type=jnp....]
  transfers between devices with their start and end apart: 5 -> 0, of which waited for: 4 -> 0; matrix products, arithmetic and copies ran while one was open for 3% -> 0% of each run, Pallas kernels for 0% -> 0%
where the time goes in v2:
time: 189 us
  Pallas kernels  185 us (98%)
  other arithmetic  2.11 us (1%)
    pallas_call x1, Pallas kernels, shards(): pl.pallas_call(step_kernel, out_shape=(jax.ShapeDtypeStruct((NC, owned, h...  185 us

profile of v2, /device:TPU:1, one launch (start us, length us, event | category | flops | bytes accessed | tf_op | source)
XLA Modules:
  0.0 189.2 jit_solution(16097894931268723942)
XLA Ops:
  0.6 0.7 multiply_add_fusion
  1.3 0.1 pad_add_fusion
  1.4 0.8 select_reduce_fusion
  2.2 0.6 compare_select_fusion.idx
  2.7 184.8 %step.1 = (f32[2,24,1024]{2,1,0:T(8,128)}, bf16[2,8,768,128]{3,2,1,0:T(8,128)(2,1)}) custom-call(s32[288]{0:T(512)} %compare_select_fusion.idx, s32[32]{0:T(128)} %inb.1, bf16[32,128,128]{2,1,0:T(8,128)(2,1)} %tiles.1, bf16[1024,768]{1,0:T(8,128)(2,1)} %feats.1, bf16[1024,1024]{1,0:T(8,128)(2,1)} %cot_in.1, bf16[24,1024]{1,0:T(8,128)(2,1)} %w_self.1, ...), custom_call_target="tpu_custom_call" | custom-call | tf_op jit(solution)/shard_map/step/pallas_call | solution.py:543
  187.5 1.6 slice_bitcast_fusion
  (1 shorter events, 0.0 us)

commit v3 on v2

--- a/solution.py
+++ b/solution.py
@@ -18,6 +18,8 @@
 BF16 = jnp.bfloat16
 
 DIST = (4, 3, 3, 2, 2, 1, 1)
+PIECES = ((0, 2), (2, 2), (4, 2), (6, 1), (7, 1))
+Z_SEM = (0, 4, 8, 9, 10, 11, 12)
 ITEMS = []
 for _i, _d in enumerate(DIST):
     ITEMS += [(_i % 2, _d), (1 - _i % 2, -_d)]
@@ -44,6 +46,10 @@
                 barrier, inc=1, device_id=moved(me, axis, by), device_id_type=MESH
             )
             count += 1
+    for by in range(1, NY):
+        other = moved(moved(me, 0, by), 1, 1)
+        pl.semaphore_signal(barrier, inc=1, device_id=other, device_id_type=MESH)
+        count += 1
     pl.semaphore_wait(barrier, count)
 
 
@@ -60,11 +66,11 @@
 def step_kernel(
     idx, inb, tiles, feats, cot_in, w_self, w_neigh, out, wg,
     ct, sl, xb, zr, zs, ibs, cot, w, pre_own, agg, left, grad,
-    out0, out1, out2, own0, own1, own2, got0, got1, got2, mid0, mid1, mid2, low0, low1, low2,
+    lp, gp, own0, own1, own2, mid0, mid1, mid2, low0, low1, low2,
     a0, a1, a2, b0, b1, b2, d0, d1, d2, every,
     x_send, x_recv, z_send, z_recv, ib_send, ib_recv, cot_sem, w_sem,
     wa_send, wa_recv, w_own, wb_send, wb_recv, wc_send, wc_recv, wd_send, wd_recv,
-    c_send, c_recv, s_send, s_recv, g_send, g_recv, p_send, p_recv,
+    l_send, l_recv, c_send, c_recv, f_send, f_recv, s_send, s_recv, g_send, g_recv,
 ):
     me = position()
     y, c, x, z = me
@@ -76,8 +82,6 @@
     rows = 32
     last = len(DIST)
     final = last - 1
-    groups = z_send.shape[1] - final
-    per = blocks // groups
 
     def at_z(by):
         return lax.rem(z + (by % NZ), NZ)
@@ -172,26 +176,28 @@
         return remote(sl.at[j, by], xb.at[j, x], send, recv, moved(me, 2, by))
 
     def x_start(j):
-        for by in (2, 1, 3):
+        for by in (1, 3, 2):
             x_copy(j, by).start()
 
     def x_wait(j):
-        for by in (2, 1, 3):
+        for by in (1, 3, 2):
             x_copy(j, by, arriving=True).wait_recv()
 
     def z_copy(d, i, g=0, arriving=False):
         if i < 2:
-            src, dst = xb.at[2 * i + d], zr.at[d, i, pl.ds(0, NX)]
+            src = sl.at[2 * i + d, 0] if g == 0 else xb.at[2 * i + d, at_x(-g)]
+            dst = zr.at[d, i, at_x(-g)]
         elif i < final:
             src, dst = zs.at[d, i - 2], zr.at[d, i]
         else:
-            piece = pl.ds(g * per, per)
+            piece = pl.ds(*PIECES[g])
             src, dst = zs.at[d, i - 2, piece], zr.at[d, i, piece]
         target = me if arriving else moved(me, 3, 1 - 2 * d)
-        return remote(src, dst, z_send.at[d, i + g], z_recv.at[d, i + g], target)
+        at = Z_SEM[i] + g
+        return remote(src, dst, z_send.at[d, at], z_recv.at[d, at], target)
 
     def pieces(i):
-        return range(groups if i == final else 1)
+        return range(NX if i < 2 else 1 if i < final else len(PIECES))
 
     def placed(at_dest, at_sender, piece, k, r):
         total = None
@@ -259,14 +265,19 @@
         x_start(j)
 
     for i in range(last):
-        for d in (0, 1):
-            x_wait(2 * i + d)
-            if i >= 2:
-                z_copy(d, i - 2, arriving=True).wait_recv()
+        if i < 2:
+            for d in (0, 1):
+                z_copy(d, i).start()
+            for by in (1, 3, 2):
+                for d in (0, 1):
+                    x_copy(2 * i + d, by, arriving=True).wait_recv()
+                    z_copy(d, i, by).start()
+        else:
+            for d in (0, 1):
+                x_wait(2 * i + d)
+                for g in pieces(i - 2):
+                    z_copy(d, i - 2, g, arriving=True).wait_recv()
                 combine(d, i)
-            if i < 2:
-                z_copy(d, i).start()
-        if i >= 2:
             for g in pieces(i):
                 for d in (0, 1):
                     z_copy(d, i, g).start()
@@ -310,28 +321,36 @@
     for d in (0, 1):
         z_copy(d, final - 1, arriving=True).wait_recv()
 
-    span = per * block
+    def swap(g, which, target):
+        here = pl.ds(PIECES[g][0] * block, PIECES[g][1] * block)
+        if which == 0:
+            src, dst = left.at[1 - c, :, here], lp.at[:, here]
+            return remote(src, dst, l_send.at[g], l_recv.at[g], target)
+        return remote(grad.at[:, here], gp.at[:, here], c_send.at[g], c_recv.at[g], target)
+
+    partner = moved(me, 1, 1)
     scale = 0.7978845608
-    for g in range(groups):
+    for g, (first, number) in enumerate(PIECES):
         for d in (0, 1):
             z_copy(d, final, g, arriving=True).wait_recv()
         for h in (0, 1):
 
-            def body(k, r, h=h):
+            def body(k, r, h=h, first=first):
                 total = placed(z, z, lambda xs: xb.at[2 * last + h, xs], k, r)
                 total += zr[h, final, k, pl.ds(r, rows), :].astype(F32)
                 total += zr[1 - h, final - 1, k, pl.ds(r, rows), :].astype(F32)
-                at = pl.multiple_of((k - g * per) * block + r, rows)
+                at = pl.multiple_of((k - first) * block + r, rows)
                 agg[pl.ds(at, rows), h * half:(h + 1) * half] = total.astype(BF16)
 
-            each_part(g * per, per, body)
-        here = pl.ds(g * span, span)
-        left[1, :, here] = agg[...].T
-
-        def gradient(n, _, here=here):
+            each_part(first, number, body)
+        span = number * block
+        here = pl.ds(first * block, span)
+        left[1, :, here] = agg[:span].T
+
+        def gradient(n, _, here=here, span=span):
             both = jnp.concatenate([w[1, 2 * n], w[1, 2 * n + 1]], axis=1)
             pre = pre_own[n, here, :]
-            pre += jnp.dot(agg[...], both, preferred_element_type=F32)
+            pre += jnp.dot(agg[:span], both, preferred_element_type=F32)
             square = pre * pre
             t = jnp.tanh(scale * (pre + 0.044715 * (square * pre)))
             slope = 0.5 * (1.0 + t)
@@ -341,42 +360,22 @@
             return 0
 
         lax.fori_loop(0, NY // 2, gradient, 0)
+        for which in (0, 1):
+            swap(g, which, partner).start()
 
     own = (own0, own1, own2)
-    outgoing = (out0, out1, out2)
-    got = (got0, got1, got2)
     parts = (own, (mid0, mid1, mid2), (low0, low1, low2))
     inbox = ((a0, a1, a2), (b0, b1, b2), (d0, d1, d2))
-
-    def terms(side, n, to):
-        both = jnp.dot(left[side], grad[n], preferred_element_type=F32)
-        for e in range(2):
-            v = both[:, e * chunk:(e + 1) * chunk].reshape(NX, NZ, 3, 8, chunk)
-            for xs in range(NX):
-                to[0][2 * n + e, :, xs] = v[xs, :, 0].astype(BF16)
-                to[1][:, 2 * n + e, xs] = v[xs, :, 1].astype(BF16)
-                to[2][xs, :, 2 * n + e] = v[xs, :, 2].astype(BF16)
-
-    def to_partner(j, n, target):
-        at = pl.ds(2 * n, 2)
-        if j == 0:
-            src, dst = out0.at[at], got0.at[at]
-        elif j == 1:
-            src, dst = out1.at[:, at], got1.at[:, at]
-        else:
-            src, dst = out2.at[:, :, at], got2.at[:, :, at]
-        return remote(src, dst, c_send.at[j, n], c_recv.at[j, n], target)
-
-    for n in range(NY // 2):
-        terms(1 - c, n, outgoing)
-        for j in range(3):
-            to_partner(j, n, moved(me, 1, 1)).start()
+    width = lp.shape[0]
 
     def own_terms(n, _):
-        terms(c, n, own)
+        pre_own[n, :width, :] = jnp.dot(left[c], grad[n], preferred_element_type=F32)
         return 0
 
     lax.fori_loop(0, NY // 2, own_terms, 0)
+    for g in range(len(PIECES)):
+        for which in (0, 1):
+            swap(g, which, me).wait_recv()
 
     def hop(j, s, by, arriving=False):
         axis = ORDER[j][s]
@@ -391,27 +390,54 @@
     def hops(j, s):
         return range(1, SIZES[ORDER[j][s]])
 
-    for j in range(3):
-        for n in range(NY // 2):
-            to_partner(j, n, me).wait_recv()
-        n1, n2 = own[j].shape[:2]
-
-        def add(n, _, j=j, n2=n2):
-            a, b = n // n2, lax.rem(n, n2)
-            own[j][a, b] = (own[j][a, b].astype(F32) + got[j][a, b].astype(F32)).astype(BF16)
-            return 0
-
-        lax.fori_loop(0, n1 * n2, add, 0)
-        for by in hops(j, 0):
-            hop(j, 0, by).start()
+    def first_hop(j, n, by, arriving=False):
+        axis = ORDER[j][0]
+        size = SIZES[axis]
+        at = me[axis]
+        there = lax.rem(at + by, size)
+        back = lax.rem(at + size - by, size) if arriving else at
+        pair = pl.ds(2 * n, 2)
+        if j == 1:
+            src, dst = own1.at[there, pair], a1.at[back, pair]
+        else:
+            src, dst = own2.at[there, :, pair], a2.at[back, :, pair]
+        target = me if arriving else moved(me, axis, by)
+        return remote(src, dst, f_send.at[j - 1, n, by - 1], f_recv.at[j - 1, n, by - 1], target)
+
+    for n in range(NY // 2):
+        both = pre_own[n, :width, :] + jnp.dot(lp[...], gp[n], preferred_element_type=F32)
+        for e in range(2):
+            v = both[:, e * chunk:(e + 1) * chunk].reshape(NX, NZ, 3, 8, chunk)
+            for xs in range(NX):
+                own1[:, 2 * n + e, xs] = v[xs, :, 1].astype(BF16)
+                own2[xs, :, 2 * n + e] = v[xs, :, 2].astype(BF16)
+                own0[2 * n + e, :, xs] = v[xs, :, 0].astype(BF16)
+        for j in (1, 2):
+            for by in hops(j, 0):
+                first_hop(j, n, by).start()
+        for there in (2 * n, 2 * n + 1):
+
+            @pl.when(y != there)
+            def _(there=there):
+                at = lax.rem(there - y + NY, NY) - 1
+                target = (there, c, x, z)
+                send, recv = s_send.at[0, 0, at], s_recv.at[0, 0, at]
+                remote(own0.at[there], a0.at[y], send, recv, target).start()
+
+    def first_hops(j):
+        return [(n, by) for n in range(NY // 2) for by in hops(j, 0)]
 
     for s in range(3):
-        for j in range(3):
+        for j in (2, 0, 1):
             axis = ORDER[j][s]
             size = SIZES[axis]
             at_axis = me[axis]
-            for by in hops(j, s):
-                hop(j, s, by, arriving=True).wait_recv()
+            if s == 0 and j > 0:
+                for n, by in first_hops(j):
+                    first_hop(j, n, by, arriving=True).wait_recv()
+            else:
+                for by in hops(j, s):
+                    hop(j, s, by, arriving=True).wait_recv()
 
             def total(at, j=j, s=s, at_axis=at_axis, size=size):
                 value = parts[s][j][(at_axis, *at)].astype(F32)
@@ -431,24 +457,29 @@
             for by in hops(j, s + 1):
                 hop(j, s + 1, by).start()
 
-    def gather(by, arriving=False):
-        dst = every.at[c, at_y(-by) if arriving else y]
-        target = me if arriving else moved(me, 0, by)
-        return remote(every.at[c, y], dst, g_send.at[by - 1], g_recv.at[by - 1], target)
-
-    for by in range(1, NY):
-        gather(by).start()
-    for by in range(1, NY):
-        gather(by, arriving=True).wait_recv()
-    pair = remote(every.at[c], every.at[c], p_send, p_recv, moved(me, 1, 1))
-    pair.start()
-    remote(every.at[c], every.at[1 - c], p_send, p_recv, me).wait_recv()
+    others = [(by, core) for by in range(NY) for core in range(NC) if by or core]
+
+    def gather(at, arriving=False):
+        by, core = others[at]
+        dst = every.at[c, y]
+        target = me
+        if arriving:
+            dst = every.at[lax.rem(c + core, NC), at_y(-by)]
+        else:
+            target = moved(moved(me, 0, by), 1, core)
+        return remote(every.at[c, y], dst, g_send.at[at], g_recv.at[at], target)
+
+    for at in range(len(others)):
+        gather(at).start()
+    for at in range(len(others)):
+        gather(at, arriving=True).wait_recv()
     for side in (0, 1):
         for n in range(NY):
             for j in range(3):
                 out[side, j * 8:(j + 1) * 8, n * chunk:(n + 1) * chunk] = every[side, n, j].astype(F32)
 
-    pair.wait_send()
+    for at in range(len(others)):
+        gather(at).wait_send()
     wd_copy.wait_send()
     for by in range(1, NZ):
         ib_copy(by).wait_send()
@@ -456,7 +487,6 @@
         wb_copy(by).wait_send()
     for by in range(1, NY):
         wc_copy(by).wait_send()
-        gather(by).wait_send()
     for j in range(len(ITEMS)):
         for by in range(1, NX):
             x_copy(j, by).wait_send()
@@ -464,12 +494,17 @@
         for d in (0, 1):
             for g in pieces(i):
                 z_copy(d, i, g).wait_send()
+    for g in range(len(PIECES)):
+        for which in (0, 1):
+            swap(g, which, partner).wait_send()
     for j in range(3):
-        for n in range(NY // 2):
-            to_partner(j, n, moved(me, 1, 1)).wait_send()
         for s in range(3):
-            for by in hops(j, s):
-                hop(j, s, by).wait_send()
+            if s == 0 and j > 0:
+                for n, by in first_hops(j):
+                    first_hop(j, n, by).wait_send()
+            else:
+                for by in hops(j, s):
+                    hop(j, s, by).wait_send()
 
 
 def shards(features, cotangent, w_self, w_neigh, tile_vals, tile_src, tile_peer, in_block):
@@ -494,7 +529,6 @@
     anywhere = pl.BlockSpec(memory_space=pl.ANY)
     steps = len(DIST)
     items = len(ITEMS)
-    groups = 4
     thirds = [(NY, NZ, NX, 8, chunk), (NZ, NY, NX, 8, chunk), (NX, NZ, NY, 8, chunk)]
     scratch = [
         pltpu.VMEM((count + 1, block, block), F32),
@@ -506,18 +540,20 @@
         pltpu.VMEM((nodes, hidden), BF16),
         pltpu.VMEM((NC, NY, width, chunk), BF16),
         pltpu.VMEM((NY // 2, nodes, 2 * chunk), F32),
-        pltpu.VMEM((nodes // groups, width), BF16),
+        pltpu.VMEM((max(n for _, n in PIECES) * block, width), BF16),
         pltpu.VMEM((2, width, nodes), BF16),
         pltpu.VMEM((NY // 2, nodes, 2 * chunk), BF16),
+        pltpu.VMEM((width, nodes), BF16),
+        pltpu.VMEM((NY // 2, nodes, 2 * chunk), BF16),
     ]
-    for skip in (0, 0, 0, 1, 2, 0, 1, 2):
+    for skip in (0, 1, 2, 0, 1, 2):
         scratch += [pltpu.VMEM(t[skip:], BF16) for t in thirds]
     scratch += [
         pltpu.VMEM((NC, NY, 3, 8, chunk), BF16),
         dma((items, NX - 1)),
         dma((items, NX - 1)),
-        dma((2, steps - 1 + groups)),
-        dma((2, steps - 1 + groups)),
+        dma((2, Z_SEM[-1] + len(PIECES))),
+        dma((2, Z_SEM[-1] + len(PIECES))),
         dma((NZ - 1,)),
         dma((NZ - 1,)),
         dma,
@@ -531,14 +567,16 @@
         dma((NY - 1,)),
         dma,
         dma,
-        dma((3, NY // 2)),
-        dma((3, NY // 2)),
+        dma((len(PIECES),)),
+        dma((len(PIECES),)),
+        dma((len(PIECES),)),
+        dma((len(PIECES),)),
+        dma((2, NY // 2, 7)),
+        dma((2, NY // 2, 7)),
         dma((3, 3, 7)),
         dma((3, 3, 7)),
-        dma((NY - 1,)),
-        dma((NY - 1,)),
-        dma,
-        dma,
+        dma((NY * NC - 1,)),
+        dma((NY * NC - 1,)),
     ]
     out, _ = pl.pallas_call(
         step_kernel,

time: 189 us -> 186 us (0.984)
  Pallas kernels: 185 us -> 181 us
    pallas_call x1, Pallas kernels: 185 us -> 181 us  [shards(): pl.pallas_call(step_kernel, out_shape=(jax.ShapeDtypeStruct((NC, owned, h...]
where the time goes in v3:
time: 186 us; the launch traced here: 185 us
  Pallas kernels  181 us (97%)
  other arithmetic  2.11 us (1%)
    pallas_call x1, Pallas kernels, shards(): pl.pallas_call(step_kernel, out_shape=(jax.ShapeDtypeStruct((NC, owned, h...  181 us

profile of v3, /device:TPU:1, one launch (start us, length us, event | category | flops | bytes accessed | tf_op | source)
XLA Modules:
  0.0 185.3 jit_solution(13060082877534959986)
XLA Ops:
  0.6 0.7 multiply_add_fusion
  1.3 0.1 pad_add_fusion
  1.4 0.8 select_reduce_fusion
  2.2 0.6 compare_select_fusion.idx
  2.7 181.0 %step.1 = (f32[2,24,1024]{2,1,0:T(8,128)}, bf16[2,8,768,128]{3,2,1,0:T(8,128)(2,1)}) custom-call(s32[288]{0:T(512)} %compare_select_fusion.idx, s32[32]{0:T(128)} %inb.1, bf16[32,128,128]{2,1,0:T(8,128)(2,1)} %tiles.1, bf16[1024,768]{1,0:T(8,128)(2,1)} %feats.1, bf16[1024,1024]{1,0:T(8,128)(2,1)} %cot_in.1, bf16[24,1024]{1,0:T(8,128)(2,1)} %w_self.1, ...), custom_call_target="tpu_custom_call" | custom-call | tf_op jit(solution)/shard_map/step/pallas_call | solution.py:581
  183.7 1.6 slice_bitcast_fusion
  (1 shorter events, 0.0 us)

commit v4 on v3

--- a/solution.py
+++ b/solution.py
@@ -281,9 +281,9 @@
             for g in pieces(i):
                 for d in (0, 1):
                     z_copy(d, i, g).start()
-        if 2 * i + 5 < len(ITEMS):
-            x_start(2 * i + 4)
-            x_start(2 * i + 5)
+        for j in range(4, 8) if i == 1 else range(2 * i + 4, 2 * i + 6) if i > 1 else ():
+            if j < len(ITEMS):
+                x_start(j)
         if i == 0:
             slots(2)
             slots(-2)

time: 186 us -> 185 us (level)
  no operation moved by 1% of the time
where the time goes in v4:
time: 185 us; the launch traced here: 184 us
  Pallas kernels  180 us (97%)
  other arithmetic  2.11 us (1%)
    pallas_call x1, Pallas kernels, shards(): pl.pallas_call(step_kernel, out_shape=(jax.ShapeDtypeStruct((NC, owned, h...  180 us

profile of v4, /device:TPU:1, one launch (start us, length us, event | category | flops | bytes accessed | tf_op | source)
XLA Modules:
  0.0 184.5 jit_solution(15960367641937004179)
XLA Ops:
  0.6 0.7 multiply_add_fusion
  1.3 0.1 pad_add_fusion
  1.4 0.8 select_reduce_fusion
  2.2 0.6 compare_select_fusion.idx
  2.7 180.1 %step.1 = (f32[2,24,1024]{2,1,0:T(8,128)}, bf16[2,8,768,128]{3,2,1,0:T(8,128)(2,1)}) custom-call(s32[288]{0:T(512)} %compare_select_fusion.idx, s32[32]{0:T(128)} %inb.1, bf16[32,128,128]{2,1,0:T(8,128)(2,1)} %tiles.1, bf16[1024,768]{1,0:T(8,128)(2,1)} %feats.1, bf16[1024,1024]{1,0:T(8,128)(2,1)} %cot_in.1, bf16[24,1024]{1,0:T(8,128)(2,1)} %w_self.1, ...), custom_call_target="tpu_custom_call" | custom-call | tf_op jit(solution)/shard_map/step/pallas_call | solution.py:581
  182.8 1.6 slice_bitcast_fusion
  (1 shorter events, 0.0 us)
